TPU v7x, 128 devices: a whole 4x4x4 slice. The times are simulated.
128 devices in a mesh: chan: 16 (over y, x), stn: 8 (over z, core).
Axes of the slice: x: 4, y: 4, z: 4, core: 2. Of those that a mesh axis runs over, the one named last changes fastest.
Arguments:
- measured_correlation: float32 [16, 8, 8192], P('chan', None, 'stn'), may hold values from -3 to 3
- model_correlation: float32 [16, 8, 16, 8192], P('chan', None, None, 'stn'), may hold values from -0.75 to 0.75
- source_pointing: int32 [16, 1], replicated, may hold values from 0 to 7
- antenna_pairs: int32 [2, 8192], P(None, 'stn'), may hold values from 0 to 511, as said below
- starting_jones_matrices: float32 [16, 8, 8, 512], P('chan'), may hold values from -1 to 2
- starting_polynomial_terms: float32 [3, 8, 8, 512], replicated, may hold values from -1 to 2
- starting_lagrange_scaled: float32 [16, 8, 8, 512], P('chan'), may hold values from -1.5 to 1.5
- augmented_lagrange_rhos: float32 [8], replicated, may hold values from 0.5 to 4
Outputs:
- solved_gains: float32 [16, 8, 8, 512], P('chan', None, None, 'stn')
- solved_dual: float32 [16, 8, 8, 512], P('chan', None, None, 'stn')
- fit_coeffs: float32 [3, 8, 8, 512], P(None, None, None, 'stn')
Inputs may be any that keep to these rules, and one draw needn't show every extreme that they name: `antenna_pairs`: row 0 holds a baseline's first station and row 1 its second, which differs from the first. The first station of every baseline in the i-th aligned block of 1024 baselines lies among stations i * 64 to (i + 1) * 64 - 1. `source_pointing`: every direction holds at least one component.
All inputs are finite; a program needn't handle non-finite values.
Results may differ from a plain program's by a relative error of at most 0.0001.
Values sent between devices are 32-bit elements; how exact they have to be, the bound alone decides.
A program may use at most 64 MiB of HBM per device.

v0:
```python
from functools import partial
import jax
import jax.numpy as jnp
from jax import lax
from jax.sharding import Mesh
from jax.sharding import PartitionSpec as P

CALIB_PATHS = 8
TERMS = 3
STEPS = 2
INNER = 2
STN = ("stn_0", "stn_1")
CHAN = ("chan_0", "chan_1")
CHAN_STN = ("chan_0", "chan_1", "stn_0", "stn_1")
student_nu = 2.0
squared_tolerance = 1e-06
highest = lax.Precision.HIGHEST


def over_axes(value, axes):
    for axis in axes:
        value = lax.psum(value, axis)
    return value


def split_up(value, dim, length):
    before, after = (value.shape[:dim], value.shape[dim + 1 :])
    return jnp.moveaxis(value.reshape(*before, length, -1, *after), dim, 0)


def sent_and_summed(value, axis, dim):
    length = lax.axis_size(axis)
    blocks = lax.all_to_all(split_up(value, dim, length), axis, 0, 0, tiled=True)
    return jnp.sum(blocks, axis=0)


def copy_for_each(value, axis):
    length = lax.axis_size(axis)
    return lax.all_to_all(
        jnp.broadcast_to(value[None], (length, *value.shape)), axis, 0, 0, tiled=True
    )


def laid_out(blocks, dim):
    blocks = jnp.moveaxis(blocks, 0, dim)
    shape = blocks.shape
    return blocks.reshape(*shape[:dim], shape[dim] * shape[dim + 1], *shape[dim + 2 :])


def gathered_copies(value, axis, dim):
    blocks = copy_for_each(value, axis)
    return laid_out(blocks, dim)


def over_pieces(value, axis):
    return lax.all_gather(value, axis).sum(0)


def entries(stacked):
    return [(stacked[slot_idx], stacked[4 + slot_idx]) for slot_idx in range(4)]


def assemble(matrix):
    return jnp.stack(
        [matrix[slot_idx][0] for slot_idx in range(4)]
        + [matrix[slot_idx][1] for slot_idx in range(4)],
        axis=0,
    )


def flatten(matrix):
    return [matrix[slot_idx][0] for slot_idx in range(4)] + [
        matrix[slot_idx][1] for slot_idx in range(4)
    ]


def multiply_pair(first_pair, second_pair):
    return (
        first_pair[0] * second_pair[0] - first_pair[1] * second_pair[1],
        first_pair[0] * second_pair[1] + first_pair[1] * second_pair[0],
    )


def add_pair(first_pair, second_pair):
    return (first_pair[0] + second_pair[0], first_pair[1] + second_pair[1])


def conjugate(value_pair):
    return (value_pair[0], -value_pair[1])


def matrix_product(factor_one, factor_two):
    return [
        add_pair(
            multiply_pair(factor_one[0], factor_two[0]), multiply_pair(factor_one[1], factor_two[2])
        ),
        add_pair(
            multiply_pair(factor_one[0], factor_two[1]), multiply_pair(factor_one[1], factor_two[3])
        ),
        add_pair(
            multiply_pair(factor_one[2], factor_two[0]), multiply_pair(factor_one[3], factor_two[2])
        ),
        add_pair(
            multiply_pair(factor_one[2], factor_two[1]), multiply_pair(factor_one[3], factor_two[3])
        ),
    ]


def adjoint(matrix):
    return [conjugate(matrix[0]), conjugate(matrix[2]), conjugate(matrix[1]), conjugate(matrix[3])]


def gram_parts(matrix):
    upper_sum = (
        matrix[0][0] * matrix[0][0]
        + matrix[0][1] * matrix[0][1]
        + matrix[1][0] * matrix[1][0]
        + matrix[1][1] * matrix[1][1]
    )
    lower_sum = (
        matrix[2][0] * matrix[2][0]
        + matrix[2][1] * matrix[2][1]
        + matrix[3][0] * matrix[3][0]
        + matrix[3][1] * matrix[3][1]
    )
    cross_term = add_pair(
        multiply_pair(matrix[0], conjugate(matrix[2])),
        multiply_pair(matrix[1], conjugate(matrix[3])),
    )
    return [upper_sum, lower_sum, cross_term[0], cross_term[1]]


def basis_table(channel_count):
    frequency = (2.0 * jnp.arange(channel_count, dtype=jnp.float32) + 1.0) / channel_count - 1.0
    columns = []
    for degree in range(TERMS):
        column = frequency**degree
        for earlier in columns:
            column = column - jnp.sum(earlier * column) / channel_count * earlier
        column = column / jnp.sqrt(jnp.sum(column * column) / channel_count)
        columns.append(column)
    return jnp.stack(columns, axis=1)


def combine_sources(cohere_f, source_pointing):
    member = (
        source_pointing[:, 0][:, None] == jnp.arange(CALIB_PATHS, dtype=jnp.int32)[None, :]
    ).astype(jnp.float32)
    return jnp.einsum("csb,sk->ckb", cohere_f, member, precision=highest)


def channel_state(vis_f, cohere_dir, spectral_jones_matrices, antenna_pairs):
    coherent = entries(cohere_dir)
    first_gain = entries(spectral_jones_matrices[:, :, antenna_pairs[0]])
    second_gain = entries(spectral_jones_matrices[:, :, antenna_pairs[1]])
    toward_first = matrix_product(coherent, adjoint(second_gain))
    own_terms = matrix_product(first_gain, toward_first)
    observed = entries(vis_f)
    residual = [
        (
            observed[slot_idx][0] - jnp.sum(own_terms[slot_idx][0], axis=0),
            observed[slot_idx][1] - jnp.sum(own_terms[slot_idx][1], axis=0),
        )
        for slot_idx in range(4)
    ]
    energy = residual[0][0] * residual[0][0] + residual[0][1] * residual[0][1]
    for slot_idx in range(1, 4):
        energy = (
            energy
            + residual[slot_idx][0] * residual[slot_idx][0]
            + residual[slot_idx][1] * residual[slot_idx][1]
        )
    return (residual, own_terms, toward_first, first_gain, coherent, energy)


def channel_sums(chan_state, weight, first_table, second_table, block_start):
    residual, own_terms, toward_first, first_gain, coherent, energy = chan_state
    target = [
        add_pair((residual[slot_idx][0][None], residual[slot_idx][1][None]), own_terms[slot_idx])
        for slot_idx in range(4)
    ]
    back_terms = matrix_product(first_gain, coherent)
    first_parts = (
        jnp.stack(
            gram_parts(toward_first) + flatten(matrix_product(target, adjoint(toward_first))),
            axis=0,
        )
        * weight
    )
    second_parts = (
        jnp.stack(
            gram_parts(adjoint(back_terms)) + flatten(matrix_product(adjoint(target), back_terms)),
            axis=0,
        )
        * weight
    )
    first_block = jnp.einsum("pkb,bs->pks", first_parts, first_table, precision=highest)
    every_station = jnp.einsum("pkb,bs->pks", second_parts, second_table, precision=highest)
    block_width = first_table.shape[1]
    own_rows = lax.dynamic_slice_in_dim(every_station, block_start, block_width, 2) + first_block
    return lax.dynamic_update_slice_in_dim(every_station, own_rows, block_start, 2)


def jones_estimator(
    least_squares_equations, pivot_spectral_point, spectral_jones_matrices, augmented_lagrange_rhos
):
    augmented_rho_factor = augmented_lagrange_rhos[:, None]
    diag_one = least_squares_equations[0] + augmented_rho_factor
    diag_two = least_squares_equations[1] + augmented_rho_factor
    determinant = (
        diag_one * diag_two
        - least_squares_equations[2] * least_squares_equations[2]
        - least_squares_equations[3] * least_squares_equations[3]
    )
    zero_part = jnp.zeros_like(determinant)
    inverse = [
        (diag_two / determinant, zero_part),
        (-least_squares_equations[2] / determinant, -least_squares_equations[3] / determinant),
        (-least_squares_equations[2] / determinant, least_squares_equations[3] / determinant),
        (diag_one / determinant, zero_part),
    ]
    right_side = entries(
        least_squares_equations[4:] + augmented_rho_factor[None] * pivot_spectral_point
    )
    solution = assemble(matrix_product(right_side, inverse))
    return 0.5 * (spectral_jones_matrices + solution)


def body(
    measured_correlation,
    model_correlation,
    source_pointing,
    antenna_pairs,
    starting_jones_matrices,
    starting_polynomial_terms,
    starting_lagrange_scaled,
    augmented_lagrange_rhos,
):
    local_ch = measured_correlation.shape[0]
    stations = starting_jones_matrices.shape[3]
    block_size = stations // lax.axis_size(STN)
    block_start = lax.axis_index(STN) * block_size
    total_ch = local_ch * lax.axis_size(CHAN)
    sample_count = total_ch * measured_correlation.shape[2] * lax.axis_size(STN)
    my_basis = lax.dynamic_slice_in_dim(
        basis_table(total_ch), lax.axis_index(CHAN) * local_ch, local_ch, 0
    )
    cohere_dir = jax.vmap(combine_sources, (0, None))(model_correlation, source_pointing)
    first_table = (
        (antenna_pairs[0] - block_start)[:, None]
        == jnp.arange(block_size, dtype=jnp.int32)[None, :]
    ).astype(jnp.float32)
    second_table = (
        antenna_pairs[1][:, None] == jnp.arange(stations, dtype=jnp.int32)[None, :]
    ).astype(jnp.float32)
    state_fn = jax.vmap(channel_state, (0, 0, 0, None))
    sums_fn = jax.vmap(
        partial(
            channel_sums,
            first_table=first_table,
            second_table=second_table,
            block_start=block_start,
        ),
        (0, 0),
    )
    estimate_routine = jax.vmap(jones_estimator, (0, 0, 0, None))

    def own_block(array):
        return lax.dynamic_slice_in_dim(array, block_start, block_size, 3)

    consensus = jnp.einsum("ft,tcks->fcks", my_basis, starting_polynomial_terms, precision=highest)
    whole_jones_matrix = starting_jones_matrices
    consensus = own_block(consensus)
    dual_now = own_block(starting_lagrange_scaled)
    gain_mine = own_block(starting_jones_matrices)
    pending = None
    fit_now = starting_polynomial_terms
    for step_idx in range(STEPS):
        pivot_antenna = consensus - dual_now
        for inner_idx in range(INNER):
            chan_state = state_fn(
                measured_correlation, cohere_dir, whole_jones_matrix, antenna_pairs
            )
            mean_square = (
                over_axes(jnp.sum(chan_state[5]), CHAN_STN) / sample_count + squared_tolerance
            )
            weight = (student_nu + 2.0) / (student_nu + chan_state[5] / mean_square)
            least_squares_equations = sums_fn(chan_state, weight)
            final_pass = step_idx == STEPS - 1 and inner_idx == INNER - 1
            block_sums = sent_and_summed(least_squares_equations, STN, 3)
            gain_mine = estimate_routine(
                block_sums, pivot_antenna, gain_mine, augmented_lagrange_rhos
            )
            if not final_pass:
                whole_jones_matrix = gathered_copies(gain_mine, STN, 3)
        partial_fit = jnp.einsum("ft,fcks->tcks", my_basis, gain_mine + dual_now, precision=highest)
        fit_now = over_pieces(partial_fit, CHAN) / total_ch
        consensus = jnp.einsum("ft,tcks->fcks", my_basis, fit_now, precision=highest)
        dual_now = dual_now + gain_mine - consensus
    return (gain_mine, dual_now, fit_now)


def solution(mesh):
    torus = Mesh(mesh.devices.reshape(4, 4, 4, 2), ("chan_0", "chan_1", "stn_0", "stn_1"))
    placed = (
        P(CHAN, None, STN),
        P(CHAN, None, None, STN),
        P(),
        P(None, STN),
        P(CHAN, None, None, None),
        P(),
        P(CHAN, None, None, None),
        P(),
    )
    return jax.shard_map(
        body,
        mesh=torus,
        in_specs=placed,
        out_specs=(P(CHAN, None, None, STN), P(CHAN, None, None, STN), P(None, None, None, STN)),
        check_vma=False,
    )
```

profile of v0, /device:TPU:0, one launch (start us, length us, event | category | flops | bytes accessed | tf_op | source)
XLA Modules:
  0.0 398.1 jit_solution(17841108396992210272)
XLA Ops:
  3.2 1.7 copy.530
  4.9 9.1 %gather_fusion.1 = f32[1024,8,8]{2,1,0:T(8,128)} fusion(f32[8,8,512]{1,0,2:T(8,128)S(1)} %bitcast.1080, s32[1024]{0:T(1024)S(1)} %get-tuple-element.366), kind=kCustom, calls=%fused_computation.1 | custom fusion | bytes 528384 | tf_op jit(solution)/shard_map/vmap()/gather | solution.py:155
  14.0 2.8 copy.543
  16.8 9.1 %gather_fusion = f32[1024,8,8]{2,1,0:T(8,128)} fusion(f32[8,8,512]{1,0,2:T(8,128)S(1)} %bitcast.1081, s32[1024]{0:T(1024)S(1)} %get-tuple-element.367), kind=kCustom, calls=%fused_computation | custom fusion | bytes 528384 | tf_op jit(solution)/shard_map/vmap()/gather | solution.py:154
  25.9 2.8 copy.531
  30.0 11.4 %psum.112 = f32[]{:T(128)} all-reduce(f32[]{:T(128)} %fusion.213), channel_id=1, replica_groups=mesh['chan_0'=4,'chan_1'=4,'stn_0'=4,'stn_1'=2] {'chan_0'}, use_global_device_ids=true, to_apply=%region_9.0 | all-reduce | flops 1 | bytes 8 | tf_op jit(solution)/shard_map/psum | solution.py:22
  41.6 11.1 %psum.113 = f32[]{:T(128)} all-reduce(f32[]{:T(128)} %psum.112), channel_id=1, replica_groups=mesh['chan_0'=4,'chan_1'=4,'stn_0'=4,'stn_1'=2] {'chan_1'}, use_global_device_ids=true, to_apply=%region_10.0 | all-reduce | flops 1 | bytes 8 | tf_op jit(solution)/shard_map/psum | solution.py:22
  53.3 12.4 %psum.114 = f32[]{:T(128)} all-reduce(f32[]{:T(128)} %psum.113), channel_id=1, replica_groups=mesh['chan_0'=4,'chan_1'=4,'stn_0'=4,'stn_1'=2] {'stn_0'}, use_global_device_ids=true, to_apply=%region_11.0 | all-reduce | flops 1 | bytes 8 | tf_op jit(solution)/shard_map/psum | solution.py:22
  66.2 3.1 psum.115
  72.4 2.2 fusion.16
  76.7 3.5 all-to-all-start
  90.5 10.7 %all_to_all.35 = f32[8,1,4096]{2,1,0:T(1,128)S(1)} all-to-all(f32[8,1,4096]{2,1,0:T(1,128)S(1)} %reshape.20802), channel_id=1, replica_groups=mesh['chan_0'=4,'chan_1'=4,'stn_0'=4,'stn_1'=2] {'stn_0','stn_1'}, dimensions={0} | all-to-all | bytes 262144 | tf_op jit(solution)/shard_map/all_to_all | solution.py:39
  103.0 9.1 %gather_fusion.3 = f32[1024,8,8]{2,1,0:T(8,128)} fusion(f32[8,8,512]{1,0,2:T(8,128)S(1)} %bitcast.1084, s32[1024]{0:T(1024)S(1)} %get-tuple-element.366), kind=kCustom, calls=%fused_computation.3 | custom fusion | bytes 528384 | tf_op jit(solution)/shard_map/vmap()/gather | solution.py:155
  112.1 9.1 %gather_fusion.2 = f32[1024,8,8]{2,1,0:T(8,128)} fusion(f32[8,8,512]{1,0,2:T(8,128)S(1)} %bitcast.1085, s32[1024]{0:T(1024)S(1)} %get-tuple-element.367), kind=kCustom, calls=%fused_computation.2 | custom fusion | bytes 528384 | tf_op jit(solution)/shard_map/vmap()/gather | solution.py:154
  121.2 2.8 copy.567
  124.1 2.8 copy.561
  127.8 8.4 %psum.116 = f32[]{:T(128)} all-reduce(f32[]{:T(128)} %fusion.212), channel_id=1, replica_groups=mesh['chan_0'=4,'chan_1'=4,'stn_0'=4,'stn_1'=2] {'chan_0'}, use_global_device_ids=true, to_apply=%region_29.0 | all-reduce | flops 1 | bytes 8 | tf_op jit(solution)/shard_map/psum | solution.py:22
  136.3 8.4 %psum.117 = f32[]{:T(128)} all-reduce(f32[]{:T(128)} %psum.116), channel_id=1, replica_groups=mesh['chan_0'=4,'chan_1'=4,'stn_0'=4,'stn_1'=2] {'chan_1'}, use_global_device_ids=true, to_apply=%region_30.0 | all-reduce | flops 1 | bytes 8 | tf_op jit(solution)/shard_map/psum | solution.py:22
  144.7 9.6 %psum.118 = f32[]{:T(128)} all-reduce(f32[]{:T(128)} %psum.117), channel_id=1, replica_groups=mesh['chan_0'=4,'chan_1'=4,'stn_0'=4,'stn_1'=2] {'stn_0'}, use_global_device_ids=true, to_apply=%region_31.0 | all-reduce | flops 1 | bytes 8 | tf_op jit(solution)/shard_map/psum | solution.py:22
  154.3 3.1 psum.119
  159.8 2.2 fusion.14
  163.3 10.1 %all_to_all.36 = f32[8,1,6144]{2,1,0:T(1,128)S(1)} all-to-all(f32[8,1,6144]{2,1,0:T(1,128)S(1)} %reshape.20804), channel_id=1, replica_groups=mesh['chan_0'=4,'chan_1'=4,'stn_0'=4,'stn_1'=2] {'stn_0','stn_1'}, dimensions={0} | all-to-all | bytes 393216 | tf_op jit(solution)/shard_map/all_to_all | solution.py:33
  176.1 3.4 all-to-all-start.3
  179.5 6.0 %all-to-all-done.3 = f32[8,1,4096]{2,1,0:T(1,128)S(1)} async-done(((f32[8,1,4096]{2,1,0:T(1,128)}), f32[8,1,4096]{2,1,0:T(1,128)S(1)}, u32[]{:S(2)}, u32[]{:S(2)}) %all-to-all-start.3) | async-done | bytes 131104 | tf_op jit(solution)/shard_map/all_to_all | solution.py:39
  187.3 9.1 %gather_fusion.5 = f32[1024,8,8]{2,1,0:T(8,128)} fusion(f32[8,8,512]{1,0,2:T(8,128)S(1)} %bitcast.1086, s32[1024]{0:T(1024)S(1)} %get-tuple-element.366), kind=kCustom, calls=%fused_computation.5 | custom fusion | bytes 528384 | tf_op jit(solution)/shard_map/vmap()/gather | solution.py:155
  196.4 9.1 %gather_fusion.4 = f32[1024,8,8]{2,1,0:T(8,128)} fusion(f32[8,8,512]{1,0,2:T(8,128)S(1)} %bitcast.1087, s32[1024]{0:T(1024)S(1)} %get-tuple-element.367), kind=kCustom, calls=%fused_computation.4 | custom fusion | bytes 528384 | tf_op jit(solution)/shard_map/vmap()/gather | solution.py:154
  205.4 2.8 copy.606
  208.3 2.8 copy.600
  212.1 24.8 %all-gather = f32[48,8,8,64]{3,2,1,0:T(8,128)S(1)} all-gather(f32[3,8,8,64]{3,2,1,0:T(8,128)S(1)} %broadcast_multiply_fusion.3), channel_id=2, replica_groups=mesh['chan_0'=4,'chan_1'=4,'stn_0'=4,'stn_1'=2] {'chan_0','chan_1'}, dimensions={0}, use_global_device_ids=true | all-gather | bytes 835584 | tf_op jit(solution)/shard_map/all_gather | solution.py:56
  236.9 10.0 %psum.120 = f32[]{:T(128)} all-reduce(f32[]{:T(128)} %fusion.211), channel_id=1, replica_groups=mesh['chan_0'=4,'chan_1'=4,'stn_0'=4,'stn_1'=2] {'chan_0'}, use_global_device_ids=true, to_apply=%region_43.0 | all-reduce | flops 1 | bytes 8 | tf_op jit(solution)/shard_map/psum | solution.py:22
  247.0 9.9 %psum.121 = f32[]{:T(128)} all-reduce(f32[]{:T(128)} %psum.120), channel_id=1, replica_groups=mesh['chan_0'=4,'chan_1'=4,'stn_0'=4,'stn_1'=2] {'chan_1'}, use_global_device_ids=true, to_apply=%region_44.0 | all-reduce | flops 1 | bytes 8 | tf_op jit(solution)/shard_map/psum | solution.py:22
  256.9 9.5 %psum.122 = f32[]{:T(128)} all-reduce(f32[]{:T(128)} %psum.121), channel_id=1, replica_groups=mesh['chan_0'=4,'chan_1'=4,'stn_0'=4,'stn_1'=2] {'stn_0'}, use_global_device_ids=true, to_apply=%region_45.0 | all-reduce | flops 1 | bytes 8 | tf_op jit(solution)/shard_map/psum | solution.py:22
  266.4 3.3 psum.123
  272.1 2.2 fusion.12
  276.3 3.5 all-to-all-start.4
  280.2 6.5 %all-to-all-done.4 = f32[8,1,6144]{2,1,0:T(1,128)S(1)} async-done(((f32[8,1,6144]{2,1,0:T(1,128)}), f32[8,1,6144]{2,1,0:T(1,128)S(1)}, u32[]{:S(2)}, u32[]{:S(2)}) %all-to-all-start.4) | async-done | bytes 196640 | tf_op jit(solution)/shard_map/all_to_all | solution.py:33
  288.5 8.6 %all_to_all.37 = f32[8,1,4096]{2,1,0:T(1,128)S(1)} all-to-all(f32[8,1,4096]{2,1,0:T(1,128)S(1)} %reshape.20810), channel_id=1, replica_groups=mesh['chan_0'=4,'chan_1'=4,'stn_0'=4,'stn_1'=2] {'stn_0','stn_1'}, dimensions={0} | all-to-all | bytes 262144 | tf_op jit(solution)/shard_map/all_to_all | solution.py:39
  298.9 9.1 %gather_fusion.7 = f32[1024,8,8]{2,1,0:T(8,128)} fusion(f32[8,8,512]{1,0,2:T(8,128)S(1)} %bitcast.1082, s32[1024]{0:T(1024)S(1)} %get-tuple-element.366), kind=kCustom, calls=%fused_computation.7 | custom fusion | bytes 528384 | tf_op jit(solution)/shard_map/vmap()/gather | solution.py:155
  308.0 9.1 %gather_fusion.6 = f32[1024,8,8]{2,1,0:T(8,128)} fusion(f32[8,8,512]{1,0,2:T(8,128)S(1)} %bitcast.1083, s32[1024]{0:T(1024)S(1)} %get-tuple-element.367), kind=kCustom, calls=%fused_computation.6 | custom fusion | bytes 528384 | tf_op jit(solution)/shard_map/vmap()/gather | solution.py:154
  317.1 2.8 copy.621
  320.0 2.8 copy.615
  323.7 8.9 %psum.124 = f32[]{:T(128)} all-reduce(f32[]{:T(128)} %fusion.210), channel_id=1, replica_groups=mesh['chan_0'=4,'chan_1'=4,'stn_0'=4,'stn_1'=2] {'chan_0'}, use_global_device_ids=true, to_apply=%region_58.0 | all-reduce | flops 1 | bytes 8 | tf_op jit(solution)/shard_map/psum | solution.py:22
  332.6 8.6 %psum.125 = f32[]{:T(128)} all-reduce(f32[]{:T(128)} %psum.124), channel_id=1, replica_groups=mesh['chan_0'=4,'chan_1'=4,'stn_0'=4,'stn_1'=2] {'chan_1'}, use_global_device_ids=true, to_apply=%region_59.0 | all-reduce | flops 1 | bytes 8 | tf_op jit(solution)/shard_map/psum | solution.py:22
  341.3 9.5 %psum.126 = f32[]{:T(128)} all-reduce(f32[]{:T(128)} %psum.125), channel_id=1, replica_groups=mesh['chan_0'=4,'chan_1'=4,'stn_0'=4,'stn_1'=2] {'stn_0'}, use_global_device_ids=true, to_apply=%region_60.0 | all-reduce | flops 1 | bytes 8 | tf_op jit(solution)/shard_map/psum | solution.py:22
  350.8 3.1 psum.127
  356.3 2.2 fusion.10
  359.9 10.1 %all_to_all.38 = f32[8,1,6144]{2,1,0:T(1,128)S(1)} all-to-all(f32[8,1,6144]{2,1,0:T(1,128)S(1)} %reshape.20812), channel_id=1, replica_groups=mesh['chan_0'=4,'chan_1'=4,'stn_0'=4,'stn_1'=2] {'stn_0','stn_1'}, dimensions={0} | all-to-all | bytes 393216 | tf_op jit(solution)/shard_map/all_to_all | solution.py:33
  372.3 24.6 %all-gather.1 = f32[48,8,8,64]{3,2,1,0:T(8,128)S(1)} all-gather(f32[3,8,8,64]{3,2,1,0:T(8,128)S(1)} %broadcast_multiply_fusion), channel_id=3, replica_groups=mesh['chan_0'=4,'chan_1'=4,'stn_0'=4,'stn_1'=2] {'chan_0','chan_1'}, dimensions={0}, use_global_device_ids=true | all-gather | bytes 835584 | tf_op jit(solution)/shard_map/all_gather | solution.py:56
  (260 shorter events, 42.6 us)
Async XLA Ops:
  0.6 28.0 %copy-start = (f32[1,8,16,1024]{3,2,1,0:T(8,128)S(1)}, f32[1,8,16,1024]{3,2,1,0:T(8,128)}, u32[]{:S(2)}) copy-start(f32[1,8,16,1024]{3,2,1,0:T(8,128)} %param.17) | copy-start | bytes 1572868
  14.0 14.7 %copy-start.10 = (s32[16,1]{0,1:T(1,128)S(1)}, s32[16,1]{0,1:T(1,128)}, u32[]{:S(2)}) copy-start(s32[16,1]{0,1:T(1,128)} %param.18) | copy-start | bytes 196
  25.9 3.5 copy-start.2
  25.9 15.6 %copy-start.11 = (s32[3]{0:T(128)S(1)}, s32[3]{0:T(128)}, u32[]{:S(2)}) copy-start(s32[3]{0:T(128)} %constant.148.clone.1) | copy-start | bytes 40
  29.2 40.9 %copy-start.9 = (s32[4]{0:T(128)S(1)}, s32[4]{0:T(128)}, u32[]{:S(2)}) copy-start(s32[4]{0:T(128)} %constant.149.clone.1) | copy-start | bytes 52
  69.5 17.3 %copy-start.3 = (f32[3,8,8,512]{3,2,1,0:T(8,128)S(1)}, f32[3,8,8,512]{3,2,1,0:T(8,128)}, u32[]{:S(2)}) copy-start(f32[3,8,8,512]{3,2,1,0:T(8,128)} %param.21) | copy-start | bytes 1179652
  69.8 20.0 %copy-start.6 = (f32[1,8,8,512]{3,2,1,0:T(8,128)S(1)}, f32[1,8,8,512]{3,2,1,0:T(8,128)}, u32[]{:S(2)}) copy-start(f32[1,8,8,512]{3,2,1,0:T(8,128)} %param.22) | copy-start | bytes 393220
  69.8 20.0 %copy-start.8 = (f32[8]{0:T(128)S(1)}, f32[8]{0:T(128)}, u32[]{:S(2)}) copy-start(f32[8]{0:T(128)} %param.23) | copy-start | bytes 100
  69.9 20.3 %copy-start.5 = (f32[1,8,8,512]{3,2,1,0:T(8,128)S(1)}, f32[1,8,8,512]{3,2,1,0:T(8,128)}, u32[]{:S(2)}) copy-start(f32[1,8,8,512]{3,2,1,0:T(8,128)} %param.20) | copy-start | bytes 393220
  76.7 11.3 %all-to-all-start = ((f32[8,1,6144]{2,1,0:T(1,128)}), f32[8,1,6144]{2,1,0:T(1,128)S(1)}, u32[]{:S(2)}, u32[]{:S(2)}) async-start(f32[8,1,6144]{2,1,0:T(1,128)} %reshape.20800), calls=%async_computation | async-start | bytes 393216 | tf_op jit(solution)/shard_map/all_to_all | solution.py:33
  176.1 9.4 %all-to-all-start.3 = ((f32[8,1,4096]{2,1,0:T(1,128)}), f32[8,1,4096]{2,1,0:T(1,128)S(1)}, u32[]{:S(2)}, u32[]{:S(2)}) async-start(f32[8,1,4096]{2,1,0:T(1,128)} %reshape.20806), calls=%async_computation.3 | async-start | bytes 262144 | tf_op jit(solution)/shard_map/all_to_all | solution.py:39
  270.8 17.2 %copy-start.7 = (f32[1,8,8,512]{3,2,1,0:T(8,128)S(1)}, f32[1,8,8,512]{3,2,1,0:T(8,128)}, u32[]{:S(2)}) copy-start(f32[1,8,8,512]{3,2,1,0:T(8,128)} %param.22) | copy-start | bytes 393220
  276.3 10.3 %all-to-all-start.4 = ((f32[8,1,6144]{2,1,0:T(1,128)}), f32[8,1,6144]{2,1,0:T(1,128)S(1)}, u32[]{:S(2)}, u32[]{:S(2)}) async-start(f32[8,1,6144]{2,1,0:T(1,128)} %reshape.20808), calls=%async_computation.4 | async-start | bytes 393216 | tf_op jit(solution)/shard_map/all_to_all | solution.py:33
  358.5 39.6 %copy-start.1 = (f32[1,8,16,1024]{3,2,1,0:T(8,128)S(1)}, f32[1,8,16,1024]{3,2,1,0:T(8,128)}, u32[]{:S(2)}) copy-start(f32[1,8,16,1024]{3,2,1,0:T(8,128)} %param.17) | copy-start | bytes 1572868
  397.0 1.0 copy-start.4
where the time goes:
time: 399 us; the launch traced here: 398 us
  blocking collectives  219 us (55%)
  local copies, waits for them, and re-layouts  111 us (28%)
  other arithmetic  22.6 us (6%)
  matrix products  14.8 us (4%)
  waiting for transfers between devices  12.4 us (3%)
  starting transfers between devices  10.4 us (3%)
  between operations  8.01 us (2%)
    psum x16, blocking collectives, over_axes(): value = lax.psum(value, axis)  130 us
    all_gather x2, blocking collectives, over_pieces(): return lax.all_gather(value, axis).sum(0)  49.3 us
    gather x8, local copies, waits for them, and re-layouts, channel_state(): second_gain = entries(spectral_jones_matrices[:, :, antenna_pairs[1]])  47.6 us
    gather x8, local copies, waits for them, and re-layouts, channel_state(): first_gain = entries(spectral_jones_matrices[:, :, antenna_pairs[0]])  47.5 us
    all_to_all x2, blocking collectives, sent_and_summed(): lax.all_to_all(split_up(value, dim, length), axis, 0, 0, tiled=True)  20.3 us
    all_to_all x2, blocking collectives, copy_for_each(): lax.all_to_all(jnp.broadcast_to(value[None], (length, *value.shape)), axi...  19.4 us
    dot_general x4, matrix products, channel_sums(): jnp.einsum('pkb,bs->pks', first_parts, first_table, precision=highest)  8.77 us
  transfers between devices with their start and end apart: 3, of which 2 were waited for; matrix products, arithmetic and copies ran while one was open for 1% of the time, Pallas kernels for 0%

commit v1 on v0

--- a/solution.py
+++ b/solution.py
@@ -19,7 +19,7 @@
 
 def over_axes(value, axes):
     for axis in axes:
-        value = lax.psum(value, axis)
+        value = jnp.sum(lax.all_gather(value, axis), axis=0)
     return value
 
 

time: 399 us -> 419 us (1.050)
  local copies, waits for them, and re-layouts: 111 us -> 135 us
  other arithmetic: 22.6 us -> 32.5 us
  blocking collectives: 219 us -> 211 us
  waiting for transfers between devices: 12.4 us -> 6.46 us
    psum x16 -> x0, blocking collectives: 130 us -> none  [over_axes(): value = lax.psum(value, axis)]
    unnamed x0 -> x16, blocking collectives: none -> 122 us
    unnamed x39 -> x83, local copies, waits for them, and re-layouts: 6.16 us -> 31 us
    reduce_sum x0 -> x16, other arithmetic: none -> 10.4 us  [over_axes(): value = jnp.sum(lax.all_gather(value, axis), axis=0)]
    all_to_all x1, waiting for transfers between devices: 5.98 us -> 0.01 us  [copy_for_each(): lax.all_to_all(jnp.broadcast_to(value[None], (length, *value.shape)), axi...]
  transfers between devices with their start and end apart: 3 -> 3, of which waited for: 2 -> 1; matrix products, arithmetic and copies ran while one was open for 1% -> 1% of each run, Pallas kernels for 0% -> 0%
where the time goes in v1:
time: 419 us; the launch traced here: 417 us
  blocking collectives  211 us (50%)
  local copies, waits for them, and re-layouts  135 us (32%)
  other arithmetic  32.5 us (8%)
  matrix products  14.3 us (3%)
  starting transfers between devices  10.4 us (2%)
  between operations  8.03 us (2%)
  waiting for transfers between devices  6.46 us (2%)
    unnamed x16, blocking collectives  122 us
    all_gather x2, blocking collectives, over_pieces(): return lax.all_gather(value, axis).sum(0)  49.8 us
    gather x8, local copies, waits for them, and re-layouts, channel_state(): second_gain = entries(spectral_jones_matrices[:, :, antenna_pairs[1]])  47.6 us
    gather x8, local copies, waits for them, and re-layouts, channel_state(): first_gain = entries(spectral_jones_matrices[:, :, antenna_pairs[0]])  47.5 us
    unnamed x83, local copies, waits for them, and re-layouts  31 us
    all_to_all x2, blocking collectives, sent_and_summed(): lax.all_to_all(split_up(value, dim, length), axis, 0, 0, tiled=True)  20.3 us
    all_to_all x2, blocking collectives, copy_for_each(): lax.all_to_all(jnp.broadcast_to(value[None], (length, *value.shape)), axi...  19.3 us
    reduce_sum x16, other arithmetic, over_axes(): value = jnp.sum(lax.all_gather(value, axis), axis=0)  10.4 us
  transfers between devices with their start and end apart: 3, of which 1 were waited for; matrix products, arithmetic and copies ran while one was open for 1% of the time, Pallas kernels for 0%

profile of v1, /device:TPU:0, one launch (start us, length us, event | category | flops | bytes accessed | tf_op | source)
XLA Modules:
  0.0 417.3 jit_solution(6593104314434414332)
XLA Ops:
  1.4 1.7 copy.530
  3.1 9.1 %gather_fusion.1 = f32[1024,8,8]{2,1,0:T(8,128)} fusion(f32[8,8,512]{1,0,2:T(8,128)S(1)} %bitcast.1100, s32[1024]{0:T(1024)S(1)} %get-tuple-element.366), kind=kCustom, calls=%fused_computation.1 | custom fusion | bytes 528384 | tf_op jit(solution)/shard_map/vmap()/gather | solution.py:155
  12.2 2.8 copy.543
  15.0 9.1 %gather_fusion = f32[1024,8,8]{2,1,0:T(8,128)} fusion(f32[8,8,512]{1,0,2:T(8,128)S(1)} %bitcast.1101, s32[1024]{0:T(1024)S(1)} %get-tuple-element.367), kind=kCustom, calls=%fused_computation | custom fusion | bytes 528384 | tf_op jit(solution)/shard_map/vmap()/gather | solution.py:154
  24.1 2.8 copy.531
  30.7 10.8 %all-reduce.1 = f32[4]{0:T(128)S(1)} all-reduce(f32[4]{0:T(128)S(1)} %dynamic-update-slice.16), channel_id=1, replica_groups=mesh['chan_0'=4,'chan_1'=4,'stn_0'=4,'stn_1'=2] {'chan_0'}, use_global_device_ids=true, to_apply=%add.1 | all-reduce | flops 4 | bytes 32
  44.1 10.5 %all-reduce.2 = f32[4]{0:T(128)S(1)} all-reduce(f32[4]{0:T(128)S(1)} %dynamic-update-slice.17), channel_id=1, replica_groups=mesh['chan_0'=4,'chan_1'=4,'stn_0'=4,'stn_1'=2] {'chan_1'}, use_global_device_ids=true, to_apply=%add.2 | all-reduce | flops 4 | bytes 32
  57.2 11.7 %all-reduce.3 = f32[4]{0:T(128)S(1)} all-reduce(f32[4]{0:T(128)S(1)} %dynamic-update-slice.18), channel_id=1, replica_groups=mesh['chan_0'=4,'chan_1'=4,'stn_0'=4,'stn_1'=2] {'stn_0'}, use_global_device_ids=true, to_apply=%add.3 | all-reduce | flops 4 | bytes 32
  71.4 2.4 all-reduce.4
  78.7 2.1 fusion.16
  82.8 3.5 all-to-all-start
  96.8 10.7 %all_to_all.35 = f32[8,1,4096]{2,1,0:T(1,128)S(1)} all-to-all(f32[8,1,4096]{2,1,0:T(1,128)S(1)} %reshape.20882), channel_id=1, replica_groups=mesh['chan_0'=4,'chan_1'=4,'stn_0'=4,'stn_1'=2] {'stn_0','stn_1'}, dimensions={0} | all-to-all | bytes 262144 | tf_op jit(solution)/shard_map/all_to_all | solution.py:39
  109.4 9.1 %gather_fusion.3 = f32[1024,8,8]{2,1,0:T(8,128)} fusion(f32[8,8,512]{1,0,2:T(8,128)S(1)} %bitcast.1104, s32[1024]{0:T(1024)S(1)} %get-tuple-element.366), kind=kCustom, calls=%fused_computation.3 | custom fusion | bytes 528384 | tf_op jit(solution)/shard_map/vmap()/gather | solution.py:155
  118.5 9.1 %gather_fusion.2 = f32[1024,8,8]{2,1,0:T(8,128)} fusion(f32[8,8,512]{1,0,2:T(8,128)S(1)} %bitcast.1105, s32[1024]{0:T(1024)S(1)} %get-tuple-element.367), kind=kCustom, calls=%fused_computation.2 | custom fusion | bytes 528384 | tf_op jit(solution)/shard_map/vmap()/gather | solution.py:154
  127.5 2.8 copy.567
  130.5 2.8 copy.561
  134.4 1.4 dynamic-update-slice.20
  135.9 7.7 %all-reduce.5 = f32[4]{0:T(128)S(1)} all-reduce(f32[4]{0:T(128)S(1)} %dynamic-update-slice.20), channel_id=1, replica_groups=mesh['chan_0'=4,'chan_1'=4,'stn_0'=4,'stn_1'=2] {'chan_0'}, use_global_device_ids=true, to_apply=%add.5 | all-reduce | flops 4 | bytes 32
  145.8 7.7 %all-reduce.6 = f32[4]{0:T(128)S(1)} all-reduce(f32[4]{0:T(128)S(1)} %dynamic-update-slice.21), channel_id=1, replica_groups=mesh['chan_0'=4,'chan_1'=4,'stn_0'=4,'stn_1'=2] {'chan_1'}, use_global_device_ids=true, to_apply=%add.6 | all-reduce | flops 4 | bytes 32
  155.7 8.9 %all-reduce.7 = f32[4]{0:T(128)S(1)} all-reduce(f32[4]{0:T(128)S(1)} %dynamic-update-slice.22), channel_id=1, replica_groups=mesh['chan_0'=4,'chan_1'=4,'stn_0'=4,'stn_1'=2] {'stn_0'}, use_global_device_ids=true, to_apply=%add.7 | all-reduce | flops 4 | bytes 32
  166.7 2.5 all-reduce.8
  171.9 2.1 fusion.14
  175.4 10.1 %all_to_all.36 = f32[8,1,6144]{2,1,0:T(1,128)S(1)} all-to-all(f32[8,1,6144]{2,1,0:T(1,128)S(1)} %reshape.20884), channel_id=1, replica_groups=mesh['chan_0'=4,'chan_1'=4,'stn_0'=4,'stn_1'=2] {'stn_0','stn_1'}, dimensions={0} | all-to-all | bytes 393216 | tf_op jit(solution)/shard_map/all_to_all | solution.py:33
  188.1 3.4 all-to-all-start.3
  191.6 25.4 %all-gather = f32[48,8,8,64]{3,2,1,0:T(8,128)S(1)} all-gather(f32[3,8,8,64]{3,2,1,0:T(8,128)S(1)} %broadcast_multiply_fusion.3), channel_id=2, replica_groups=mesh['chan_0'=4,'chan_1'=4,'stn_0'=4,'stn_1'=2] {'chan_0','chan_1'}, dimensions={0}, use_global_device_ids=true | all-gather | bytes 835584 | tf_op jit(solution)/shard_map/all_gather | solution.py:56
  218.9 9.1 %gather_fusion.5 = f32[1024,8,8]{2,1,0:T(8,128)} fusion(f32[8,8,512]{1,0,2:T(8,128)S(1)} %bitcast.1106, s32[1024]{0:T(1024)S(1)} %get-tuple-element.366), kind=kCustom, calls=%fused_computation.5 | custom fusion | bytes 528384 | tf_op jit(solution)/shard_map/vmap()/gather | solution.py:155
  228.0 9.1 %gather_fusion.4 = f32[1024,8,8]{2,1,0:T(8,128)} fusion(f32[8,8,512]{1,0,2:T(8,128)S(1)} %bitcast.1107, s32[1024]{0:T(1024)S(1)} %get-tuple-element.367), kind=kCustom, calls=%fused_computation.4 | custom fusion | bytes 528384 | tf_op jit(solution)/shard_map/vmap()/gather | solution.py:154
  237.1 2.8 copy.606
  240.0 2.8 copy.600
  245.5 9.3 %all-reduce.9 = f32[4]{0:T(128)S(1)} all-reduce(f32[4]{0:T(128)S(1)} %dynamic-update-slice.24), channel_id=1, replica_groups=mesh['chan_0'=4,'chan_1'=4,'stn_0'=4,'stn_1'=2] {'chan_0'}, use_global_device_ids=true, to_apply=%add.9 | all-reduce | flops 4 | bytes 32
  257.0 9.4 %all-reduce.10 = f32[4]{0:T(128)S(1)} all-reduce(f32[4]{0:T(128)S(1)} %dynamic-update-slice.25), channel_id=1, replica_groups=mesh['chan_0'=4,'chan_1'=4,'stn_0'=4,'stn_1'=2] {'chan_1'}, use_global_device_ids=true, to_apply=%add.10 | all-reduce | flops 4 | bytes 32
  268.5 10.5 %all-reduce.11 = f32[4]{0:T(128)S(1)} all-reduce(f32[4]{0:T(128)S(1)} %dynamic-update-slice.26), channel_id=1, replica_groups=mesh['chan_0'=4,'chan_1'=4,'stn_0'=4,'stn_1'=2] {'stn_0'}, use_global_device_ids=true, to_apply=%add.11 | all-reduce | flops 4 | bytes 32
  281.1 2.5 all-reduce.12
  286.3 2.1 fusion.12
  290.4 3.5 all-to-all-start.4
  294.3 6.5 %all-to-all-done.4 = f32[8,1,6144]{2,1,0:T(1,128)S(1)} async-done(((f32[8,1,6144]{2,1,0:T(1,128)}), f32[8,1,6144]{2,1,0:T(1,128)S(1)}, u32[]{:S(2)}, u32[]{:S(2)}) %all-to-all-start.4) | async-done | bytes 196640 | tf_op jit(solution)/shard_map/all_to_all | solution.py:33
  302.7 8.5 %all_to_all.37 = f32[8,1,4096]{2,1,0:T(1,128)S(1)} all-to-all(f32[8,1,4096]{2,1,0:T(1,128)S(1)} %reshape.20890), channel_id=1, replica_groups=mesh['chan_0'=4,'chan_1'=4,'stn_0'=4,'stn_1'=2] {'stn_0','stn_1'}, dimensions={0} | all-to-all | bytes 262144 | tf_op jit(solution)/shard_map/all_to_all | solution.py:39
  313.0 9.1 %gather_fusion.7 = f32[1024,8,8]{2,1,0:T(8,128)} fusion(f32[8,8,512]{1,0,2:T(8,128)S(1)} %bitcast.1102, s32[1024]{0:T(1024)S(1)} %get-tuple-element.366), kind=kCustom, calls=%fused_computation.7 | custom fusion | bytes 528384 | tf_op jit(solution)/shard_map/vmap()/gather | solution.py:155
  322.1 9.1 %gather_fusion.6 = f32[1024,8,8]{2,1,0:T(8,128)} fusion(f32[8,8,512]{1,0,2:T(8,128)S(1)} %bitcast.1103, s32[1024]{0:T(1024)S(1)} %get-tuple-element.367), kind=kCustom, calls=%fused_computation.6 | custom fusion | bytes 528384 | tf_op jit(solution)/shard_map/vmap()/gather | solution.py:154
  331.1 2.8 copy.621
  334.1 2.8 copy.615
  339.5 8.5 %all-reduce.13 = f32[4]{0:T(128)S(1)} all-reduce(f32[4]{0:T(128)S(1)} %dynamic-update-slice.28), channel_id=1, replica_groups=mesh['chan_0'=4,'chan_1'=4,'stn_0'=4,'stn_1'=2] {'chan_0'}, use_global_device_ids=true, to_apply=%add.13 | all-reduce | flops 4 | bytes 32
  350.0 7.8 %all-reduce.14 = f32[4]{0:T(128)S(1)} all-reduce(f32[4]{0:T(128)S(1)} %dynamic-update-slice.29), channel_id=1, replica_groups=mesh['chan_0'=4,'chan_1'=4,'stn_0'=4,'stn_1'=2] {'chan_1'}, use_global_device_ids=true, to_apply=%add.14 | all-reduce | flops 4 | bytes 32
  359.8 8.9 %all-reduce.15 = f32[4]{0:T(128)S(1)} all-reduce(f32[4]{0:T(128)S(1)} %dynamic-update-slice.30), channel_id=1, replica_groups=mesh['chan_0'=4,'chan_1'=4,'stn_0'=4,'stn_1'=2] {'stn_0'}, use_global_device_ids=true, to_apply=%add.15 | all-reduce | flops 4 | bytes 32
  370.7 2.5 all-reduce.16
  375.8 2.1 fusion.10
  379.3 10.1 %all_to_all.38 = f32[8,1,6144]{2,1,0:T(1,128)S(1)} all-to-all(f32[8,1,6144]{2,1,0:T(1,128)S(1)} %reshape.20892), channel_id=1, replica_groups=mesh['chan_0'=4,'chan_1'=4,'stn_0'=4,'stn_1'=2] {'stn_0','stn_1'}, dimensions={0} | all-to-all | bytes 393216 | tf_op jit(solution)/shard_map/all_to_all | solution.py:33
  391.8 24.4 %all-gather.1 = f32[48,8,8,64]{3,2,1,0:T(8,128)S(1)} all-gather(f32[3,8,8,64]{3,2,1,0:T(8,128)S(1)} %broadcast_multiply_fusion), channel_id=3, replica_groups=mesh['chan_0'=4,'chan_1'=4,'stn_0'=4,'stn_1'=2] {'chan_0','chan_1'}, dimensions={0}, use_global_device_ids=true | all-gather | bytes 835584 | tf_op jit(solution)/shard_map/all_gather | solution.py:56
  (320 shorter events, 75.1 us)
Async XLA Ops:
  0.6 26.3 %copy-start = (f32[1,8,16,1024]{3,2,1,0:T(8,128)S(1)}, f32[1,8,16,1024]{3,2,1,0:T(8,128)}, u32[]{:S(2)}) copy-start(f32[1,8,16,1024]{3,2,1,0:T(8,128)} %param.17) | copy-start | bytes 1572868
  12.2 14.8 %copy-start.10 = (s32[16,1]{0,1:T(1,128)S(1)}, s32[16,1]{0,1:T(1,128)}, u32[]{:S(2)}) copy-start(s32[16,1]{0,1:T(1,128)} %param.18) | copy-start | bytes 196
  24.1 3.6 copy-start.2
  26.9 1.2 copy-start.15
  26.9 14.6 %copy-start.14 = (u32[128]{0:T(128)S(1)}, u32[128]{0:T(128)}, u32[]{:S(2)}) copy-start(u32[128]{0:T(128)} %constant.247) | copy-start | bytes 1540
  26.9 27.6 %copy-start.13 = (u32[128]{0:T(128)S(1)}, u32[128]{0:T(128)}, u32[]{:S(2)}) copy-start(u32[128]{0:T(128)} %constant.252) | copy-start | bytes 1540
  27.0 41.9 %copy-start.12 = (u32[128]{0:T(128)S(1)}, u32[128]{0:T(128)}, u32[]{:S(2)}) copy-start(u32[128]{0:T(128)} %constant.257) | copy-start | bytes 1540
  27.5 46.8 %copy-start.8 = (s32[2,1024]{1,0:T(2,128)S(1)}, s32[2,1024]{1,0:T(2,128)}, u32[]{:S(2)}) copy-start(s32[2,1024]{1,0:T(2,128)} %param.19) | copy-start | bytes 24580
  27.5 46.9 %copy-start.11 = (s32[3]{0:T(128)S(1)}, s32[3]{0:T(128)}, u32[]{:S(2)}) copy-start(s32[3]{0:T(128)} %constant.148.clone.1) | copy-start | bytes 40
  27.5 49.5 %copy-start.9 = (s32[4]{0:T(128)S(1)}, s32[4]{0:T(128)}, u32[]{:S(2)}) copy-start(s32[4]{0:T(128)} %constant.149.clone.1) | copy-start | bytes 52
  28.0 65.0 %copy-start.3 = (f32[3,8,8,512]{3,2,1,0:T(8,128)S(1)}, f32[3,8,8,512]{3,2,1,0:T(8,128)}, u32[]{:S(2)}) copy-start(f32[3,8,8,512]{3,2,1,0:T(8,128)} %param.21) | copy-start | bytes 1179652
  74.0 22.1 %copy-start.6 = (f32[1,8,8,512]{3,2,1,0:T(8,128)S(1)}, f32[1,8,8,512]{3,2,1,0:T(8,128)}, u32[]{:S(2)}) copy-start(f32[1,8,8,512]{3,2,1,0:T(8,128)} %param.22) | copy-start | bytes 393220
  74.0 22.1 %copy-start.7 = (f32[8]{0:T(128)S(1)}, f32[8]{0:T(128)}, u32[]{:S(2)}) copy-start(f32[8]{0:T(128)} %param.23) | copy-start | bytes 100
  74.1 22.4 %copy-start.5 = (f32[1,8,8,512]{3,2,1,0:T(8,128)S(1)}, f32[1,8,8,512]{3,2,1,0:T(8,128)}, u32[]{:S(2)}) copy-start(f32[1,8,8,512]{3,2,1,0:T(8,128)} %param.20) | copy-start | bytes 393220
  82.8 11.4 %all-to-all-start = ((f32[8,1,6144]{2,1,0:T(1,128)}), f32[8,1,6144]{2,1,0:T(1,128)S(1)}, u32[]{:S(2)}, u32[]{:S(2)}) async-start(f32[8,1,6144]{2,1,0:T(1,128)} %reshape.20880), calls=%async_computation | async-start | bytes 393216 | tf_op jit(solution)/shard_map/all_to_all | solution.py:33
  188.1 29.0 %all-to-all-start.3 = ((f32[8,1,4096]{2,1,0:T(1,128)}), f32[8,1,4096]{2,1,0:T(1,128)S(1)}, u32[]{:S(2)}, u32[]{:S(2)}) async-start(f32[8,1,4096]{2,1,0:T(1,128)} %reshape.20886), calls=%async_computation.3 | async-start | bytes 262144 | tf_op jit(solution)/shard_map/all_to_all | solution.py:39
  290.4 10.3 %all-to-all-start.4 = ((f32[8,1,6144]{2,1,0:T(1,128)}), f32[8,1,6144]{2,1,0:T(1,128)S(1)}, u32[]{:S(2)}, u32[]{:S(2)}) async-start(f32[8,1,6144]{2,1,0:T(1,128)} %reshape.20888), calls=%async_computation.4 | async-start | bytes 393216 | tf_op jit(solution)/shard_map/all_to_all | solution.py:33
  377.9 39.4 %copy-start.1 = (f32[1,8,16,1024]{3,2,1,0:T(8,128)S(1)}, f32[1,8,16,1024]{3,2,1,0:T(8,128)}, u32[]{:S(2)}) copy-start(f32[1,8,16,1024]{3,2,1,0:T(8,128)} %param.17) | copy-start | bytes 1572868
  416.3 1.0 copy-start.4
